TPU v7x, 32 devices: a whole 2x2x4 slice. The times are simulated.
32 devices in a mesh: replica: 2 (over y), fsdp: 16 (over z, x, core).
Axes of the slice: x: 2, y: 2, z: 4, core: 2. Of those that a mesh axis runs over, the one named last changes fastest.
Arguments:
- tokens: float32 [6144, 768], P(('replica', 'fsdp')), may hold values from -6 to 6
- segment: int32 [32, 192], P(('replica', 'fsdp')), may hold values from 0 to 7, never falling along the last dimension, each value on 1 to 96 neighbouring positions
- cotangent: float32 [6144, 768], P(('replica', 'fsdp')), may hold values from -6 to 6
- norm1_gain: bfloat16 [768], P('fsdp'), may hold values from 0.5 to 1.5
- norm1_shift: bfloat16 [768], P('fsdp'), may hold values from -1 to 1
- qkv_weight: bfloat16 [768, 2304], P('fsdp'), may hold values from -2 to 2
- qv_bias: bfloat16 [1536], P('fsdp'), may hold values from -1 to 1
- out_weight: bfloat16 [768, 768], P('fsdp'), may hold values from -0.625 to 0.625
- out_bias: bfloat16 [768], P('fsdp'), may hold values from -1 to 1
- norm2_gain: bfloat16 [768], P('fsdp'), may hold values from 0.5 to 1.5
- norm2_shift: bfloat16 [768], P('fsdp'), may hold values from -1 to 1
- fc1_weight: bfloat16 [768, 3072], P('fsdp'), may hold values from -0.109375 to 0.109375
- fc1_bias: bfloat16 [3072], P('fsdp'), may hold values from -1.4 to 1.4
- fc2_weight: bfloat16 [3072, 768], P('fsdp'), may hold values from -0.15625 to 0.15625
- fc2_bias: bfloat16 [768], P('fsdp'), may hold values from -1 to 1
Outputs:
- layer_out: float32 [6144, 768], P(('replica', 'fsdp'))
- grad_tokens: float32 [6144, 768], P(('replica', 'fsdp'))
- grad_norm1_gain: float32 [768], P('fsdp')
- grad_norm1_shift: float32 [768], P('fsdp')
- grad_qkv_weight: float32 [768, 2304], P('fsdp')
- grad_qv_bias: float32 [1536], P('fsdp')
- grad_out_weight: float32 [768, 768], P('fsdp')
- grad_out_bias: float32 [768], P('fsdp')
- grad_norm2_gain: float32 [768], P('fsdp')
- grad_norm2_shift: float32 [768], P('fsdp')
- grad_fc1_weight: float32 [768, 3072], P('fsdp')
- grad_fc1_bias: float32 [3072], P('fsdp')
- grad_fc2_weight: float32 [3072, 768], P('fsdp')
- grad_fc2_bias: float32 [768], P('fsdp')
Inputs may be any that keep to these rules, and one draw needn't show every extreme that they name: `segment`: along each sequence the numbers never fall; a run of equal numbers is one document.
All inputs are finite; a program needn't handle non-finite values.
Results may differ from a plain program's by a relative error of at most 0.025.
The roundings to bfloat16 on the way count: a program that leaves them out, or rounds other values in their place, can miss the bound.
Values may be sent and summed in bfloat16 or wider, within the bound.
No kernel may reach another device: no remote copies, remote signals or barrier semaphores. Data moves between devices by JAX's collectives and lax.ppermute only.
A program may use at most 128 MiB of HBM per device.

v0:
```python
import jax
import jax.numpy as jnp
from jax import lax
from jax.sharding import PartitionSpec as P

D = 768
HEADS = 12
HEAD_DIM = 64
L = 192
EPSILON = 1e-05


def layer_norm(inputs, gain_vec, shift_vec):
    average = jnp.mean(inputs, axis=-1, keepdims=True)
    centered = inputs - average
    variance = jnp.mean(centered * centered, axis=-1, keepdims=True)
    inv_std = lax.rsqrt(variance + EPSILON)
    normed = centered * inv_std
    return (normed * gain_vec.astype(jnp.float32) + shift_vec.astype(jnp.float32), normed, inv_std)


def norm_back(grad_out, normed, inv_std, gain_vec):
    grad_norm = grad_out * gain_vec.astype(jnp.float32)
    first = jnp.mean(grad_norm, axis=-1, keepdims=True)
    second = jnp.mean(grad_norm * normed, axis=-1, keepdims=True)
    grad_in = inv_std * (grad_norm - first - normed * second)
    return (grad_in, jnp.sum(grad_out * normed, axis=0), jnp.sum(grad_out, axis=0))


def allowed_pairs(segment):
    length = segment.shape[1]
    causal = jnp.arange(length)[:, None] >= jnp.arange(length)[None, :]
    same_doc = segment[:, :, None] == segment[:, None, :]
    return (same_doc & causal[None])[:, None]


def masked_scores(queries, key_rows, allowed):
    scores = jnp.einsum(
        "bqhe,bkhe->bhqk", queries, key_rows, preferred_element_type=jnp.float32
    ) * HEAD_DIM ** (-0.5)
    return jnp.where(allowed, scores, -1e30)


def on_device(
    tokens,
    segment,
    cotangent,
    norm1_gain,
    norm1_shift,
    qkv_weight,
    qv_bias,
    out_weight,
    out_bias,
    norm2_gain,
    norm2_shift,
    fc1_weight,
    fc1_bias,
    fc2_weight,
    fc2_bias,
):
    f32 = jnp.float32
    bf16 = jnp.bfloat16
    seq_count = segment.shape[0]
    row_count = tokens.shape[0]
    gathered = (
        lax.all_gather(norm1_gain, "fsdp", axis=0, tiled=True),
        lax.all_gather(norm1_shift, "fsdp", axis=0, tiled=True),
        lax.all_gather(qkv_weight, "fsdp", axis=0, tiled=True),
        lax.all_gather(qv_bias, "fsdp", axis=0, tiled=True),
        lax.all_gather(out_weight, "fsdp", axis=0, tiled=True),
        lax.all_gather(out_bias, "fsdp", axis=0, tiled=True),
        lax.all_gather(norm2_gain, "fsdp", axis=0, tiled=True),
        lax.all_gather(norm2_shift, "fsdp", axis=0, tiled=True),
        lax.all_gather(fc1_weight, "fsdp", axis=0, tiled=True),
        lax.all_gather(fc1_bias, "fsdp", axis=0, tiled=True),
        lax.all_gather(fc2_weight, "fsdp", axis=0, tiled=True),
        lax.all_gather(fc2_bias, "fsdp", axis=0, tiled=True),
    )
    (
        gain_one,
        shift_one,
        qkv_full,
        qv_full,
        out_full,
        out_bias_full,
        gain_two,
        shift_two,
        up_full,
        up_bias_full,
        down_full,
        down_bias_full,
    ) = gathered
    normed1, hat_one, rstd_one = layer_norm(tokens, gain_one, shift_one)
    n_one = normed1.astype(bf16)
    proj = jnp.dot(n_one, qkv_full, preferred_element_type=f32)
    qv_f = qv_full.astype(f32)
    queries = (proj[:, :D] + qv_f[:D]).astype(bf16).reshape(seq_count, L, HEADS, HEAD_DIM)
    key_rows = proj[:, D : 2 * D].astype(bf16).reshape(seq_count, L, HEADS, HEAD_DIM)
    values = (proj[:, 2 * D :] + qv_f[D:]).astype(bf16).reshape(seq_count, L, HEADS, HEAD_DIM)
    allowed = allowed_pairs(segment)
    scores = masked_scores(queries, key_rows, allowed)
    top = jnp.max(scores, axis=-1, keepdims=True)
    log_total = top + jnp.log(jnp.sum(jnp.exp(scores - top), axis=-1, keepdims=True))
    probs_b = jnp.where(allowed, jnp.exp(scores - log_total), 0.0).astype(bf16)
    attn = jnp.einsum("bhqk,bkhe->bqhe", probs_b, values, preferred_element_type=f32)
    attn = attn.reshape(row_count, D).astype(bf16)
    resid = tokens + jnp.dot(attn, out_full, preferred_element_type=f32) + out_bias_full.astype(f32)
    normed2, hat_two, rstd_two = layer_norm(resid, gain_two, shift_two)
    n_two = normed2.astype(bf16)
    pre = jnp.dot(n_two, up_full, preferred_element_type=f32) + up_bias_full.astype(f32)
    act = jnp.maximum(pre, 0.0).astype(bf16)
    layer_out = (
        resid + jnp.dot(act, down_full, preferred_element_type=f32) + down_bias_full.astype(f32)
    )
    again = (
        lax.all_gather(norm1_gain, "fsdp", axis=0, tiled=True),
        lax.all_gather(norm1_shift, "fsdp", axis=0, tiled=True),
        lax.all_gather(qkv_weight, "fsdp", axis=0, tiled=True),
        lax.all_gather(qv_bias, "fsdp", axis=0, tiled=True),
        lax.all_gather(out_weight, "fsdp", axis=0, tiled=True),
        lax.all_gather(out_bias, "fsdp", axis=0, tiled=True),
        lax.all_gather(norm2_gain, "fsdp", axis=0, tiled=True),
        lax.all_gather(norm2_shift, "fsdp", axis=0, tiled=True),
        lax.all_gather(fc1_weight, "fsdp", axis=0, tiled=True),
        lax.all_gather(fc1_bias, "fsdp", axis=0, tiled=True),
        lax.all_gather(fc2_weight, "fsdp", axis=0, tiled=True),
        lax.all_gather(fc2_bias, "fsdp", axis=0, tiled=True),
    )
    (
        gain_one,
        shift_one,
        qkv_full,
        qv_full,
        out_full,
        out_bias_full,
        gain_two,
        shift_two,
        up_full,
        up_bias_full,
        down_full,
        down_bias_full,
    ) = again
    cot_b = cotangent.astype(bf16)
    g_fc2_b = jnp.sum(cotangent, axis=0)
    d_act = jnp.dot(cot_b, down_full.T, preferred_element_type=f32)
    d_pre = jnp.where(pre > 0, d_act, 0.0)
    g_fc1_b = jnp.sum(d_pre, axis=0)
    d_pre_b = d_pre.astype(bf16)
    d_normed2 = jnp.dot(d_pre_b, up_full.T, preferred_element_type=f32)
    d_two, g_gain_two, g_shift_two = norm_back(d_normed2, hat_two, rstd_two, gain_two)
    d_resid = cotangent + d_two
    d_resid_b = d_resid.astype(bf16)
    g_out_b = jnp.sum(d_resid, axis=0)
    d_attn = jnp.dot(d_resid_b, out_full.T, preferred_element_type=f32).astype(bf16)
    d_attn = d_attn.reshape(seq_count, L, HEADS, HEAD_DIM)
    scores = masked_scores(queries, key_rows, allowed)
    probs = jnp.where(allowed, jnp.exp(scores - log_total), 0.0)
    probs_b = probs.astype(bf16)
    d_values = jnp.einsum("bhqk,bqhe->bkhe", probs_b, d_attn, preferred_element_type=f32)
    d_probs = jnp.einsum("bqhe,bkhe->bhqk", d_attn, values, preferred_element_type=f32)
    delta = jnp.sum(probs * d_probs, axis=-1, keepdims=True)
    d_scores = (probs * (d_probs - delta) * HEAD_DIM ** (-0.5)).astype(bf16)
    d_queries = jnp.einsum(
        "bhqk,bkhe->bqhe", d_scores, key_rows, preferred_element_type=f32
    ).reshape(row_count, D)
    d_keys = jnp.einsum("bhqk,bqhe->bkhe", d_scores, queries, preferred_element_type=f32).reshape(
        row_count, D
    )
    d_values = d_values.reshape(row_count, D)
    g_qv_b = jnp.concatenate([jnp.sum(d_queries, axis=0), jnp.sum(d_values, axis=0)])
    d_proj = jnp.concatenate([d_queries, d_keys, d_values], axis=1).astype(bf16)
    d_normed1 = jnp.dot(d_proj, qkv_full.T, preferred_element_type=f32)
    d_one, g_gain_one, g_shift_one = norm_back(d_normed1, hat_one, rstd_one, gain_one)
    grad_tokens = d_resid + d_one
    replicas = lax.axis_size("replica")
    owners = lax.axis_size("fsdp")
    factor = (row_count * replicas * owners) ** (-0.5)
    operand_pairs = ((n_one, d_proj), (attn, d_resid_b), (n_two, d_pre_b), (act, cot_b))
    mats = tuple(
        (
            jnp.dot(left.T, right, preferred_element_type=f32) * factor
            for left, right in operand_pairs
        )
    )
    owned = (
        lax.psum_scatter(g_gain_one * factor, "fsdp", scatter_dimension=0, tiled=True),
        lax.psum_scatter(g_shift_one * factor, "fsdp", scatter_dimension=0, tiled=True),
        lax.psum_scatter(mats[0], "fsdp", scatter_dimension=0, tiled=True),
        lax.psum_scatter(g_qv_b * factor, "fsdp", scatter_dimension=0, tiled=True),
        lax.psum_scatter(mats[1], "fsdp", scatter_dimension=0, tiled=True),
        lax.psum_scatter(g_out_b * factor, "fsdp", scatter_dimension=0, tiled=True),
        lax.psum_scatter(g_gain_two * factor, "fsdp", scatter_dimension=0, tiled=True),
        lax.psum_scatter(g_shift_two * factor, "fsdp", scatter_dimension=0, tiled=True),
        lax.psum_scatter(mats[2], "fsdp", scatter_dimension=0, tiled=True),
        lax.psum_scatter(g_fc1_b * factor, "fsdp", scatter_dimension=0, tiled=True),
        lax.psum_scatter(mats[3], "fsdp", scatter_dimension=0, tiled=True),
        lax.psum_scatter(g_fc2_b * factor, "fsdp", scatter_dimension=0, tiled=True),
    )
    summed = lax.psum(
        (
            owned[0],
            owned[1],
            owned[2],
            owned[3],
            owned[4],
            owned[5],
            owned[6],
            owned[7],
            owned[8],
            owned[9],
            owned[10],
            owned[11],
        ),
        "replica",
    )
    return (layer_out, grad_tokens) + tuple(summed)


def solution(mesh):
    in_specs = (
        P(("replica", "fsdp"), None),
        P(("replica", "fsdp"), None),
        P(("replica", "fsdp"), None),
        P("fsdp"),
        P("fsdp"),
        P("fsdp", None),
        P("fsdp"),
        P("fsdp", None),
        P("fsdp"),
        P("fsdp"),
        P("fsdp"),
        P("fsdp", None),
        P("fsdp"),
        P("fsdp", None),
        P("fsdp"),
    )
    out_specs = (
        P(("replica", "fsdp"), None),
        P(("replica", "fsdp"), None),
        P("fsdp"),
        P("fsdp"),
        P("fsdp", None),
        P("fsdp"),
        P("fsdp", None),
        P("fsdp"),
        P("fsdp"),
        P("fsdp"),
        P("fsdp", None),
        P("fsdp"),
        P("fsdp", None),
        P("fsdp"),
    )
    return jax.shard_map(
        on_device, mesh=mesh, in_specs=in_specs, out_specs=out_specs, check_vma=False
    )
```

profile of v0, /device:TPU:0, one launch (start us, length us, event | category | flops | bytes accessed | tf_op | source)
XLA Modules:
  0.0 705.3 jit_solution(12150744632459119481)
XLA Ops:
  20.0 63.9 %all-reduce.19 = (bf16[768]{0:T(1024)(128)(2,1)S(1)}, bf16[768]{0:T(1024)(128)(2,1)S(1)}, bf16[1536]{0:T(1024)(128)(2,1)S(1)}, bf16[768]{0:T(1024)(128)(2,1)S(1)...) all-reduce(bf16[768]{0:T(1024)(128)(2,1)S(1)} %dynamic-update-slice, ...), channel_id=1, replica_groups=mesh['replica'=2,'fsdp'=16] {'fsdp'}, use_global_device_ids=true, to_apply=%add.1 | all-reduce | flops 9216 | bytes 36864
  88.0 2.9 fusion.42
  94.4 5.4 all-gather.7.cloned.1.call-done
  99.8 1.8 fusion.48
  102.4 51.7 %all-gather.9.cloned.1.call-done = bf16[768,3072]{1,0:T(8,128)(2,1)} async-done(((bf16[48,3072]{1,0:T(8,128)(2,1)}), bf16[768,3072]{1,0:T(8,128)(2,1)}) %all-gather.9.cloned.1.call-update) | async-done | bytes 4718608 | tf_op jit(solution)/shard_map/all_gather | solution.py:74
  154.1 3.5 convolution_add_fusion
  157.6 50.3 %all-gather.11.cloned.1.call-done = bf16[3072,768]{1,0:T(8,128)(2,1)} async-done(((bf16[192,768]{1,0:T(8,128)(2,1)}), bf16[3072,768]{1,0:T(8,128)(2,1)}) %all-gather.11.cloned.1.call-update) | async-done | bytes 4718608 | tf_op jit(solution)/shard_map/all_gather | solution.py:76
  208.0 4.9 fusion.51
  212.9 2.4 multiply_reduce_fusion.1
  217.0 1.9 convolution_multiply_fusion.3
  219.1 2.8 convolution_convert_fusion.1
  221.9 1.9 copy.53
  223.8 3.1 fusion.52
  226.9 6.5 fusion.15
  233.4 7.0 fusion.44
  240.4 3.3 fusion.45
  244.4 4.2 convolution_multiply_fusion
  249.3 6.5 convolution_multiply_fusion.2
  255.9 6.2 convolution_multiply_fusion.1
  264.8 1.4 reduce_sum.190
  267.5 5.2 multiply_reduce_fusion.2
  275.1 5.8 reduce-scatter.7.cloned.1.call-done
  280.8 92.9 %reduce-scatter.5.cloned.1.call-done = f32[48,2304]{1,0:T(8,128)} async-done(((f32[768,2304]{1,0:T(8,128)}), f32[48,2304]{1,0:T(8,128)}) %reduce-scatter.5.cloned.1.call-update) | async-done | bytes 442384 | tf_op jit(solution)/shard_map/reduce_scatter | solution.py:188
  373.7 115.0 %reduce-scatter.9.cloned.1.call-done = f32[48,3072]{1,0:T(8,128)} async-done(((f32[768,3072]{1,0:T(8,128)}), f32[48,3072]{1,0:T(8,128)}) %reduce-scatter.9.cloned.1.call-update) | async-done | bytes 589840 | tf_op jit(solution)/shard_map/reduce_scatter | solution.py:194
  488.7 115.0 %reduce-scatter.11.cloned.1.call-done = f32[192,768]{1,0:T(8,128)} async-done(((f32[3072,768]{1,0:T(8,128)}), f32[192,768]{1,0:T(8,128)}) %reduce-scatter.11.cloned.1.call-update) | async-done | bytes 589840 | tf_op jit(solution)/shard_map/reduce_scatter | solution.py:196
  607.5 61.4 %all-reduce.16 = (f32[768]{0:T(1024)}, f32[768]{0:T(1024)}, f32[1536]{0:T(1024)}, f32[768]{0:T(1024)}, f32[768]{0:T(1024)}, /*index=5*/f32[768]{0:T(1024)}, f32[3072]{0:T(1024)}, f32[768]{0:T(1024)}) all-reduce(f32[768]{0:T(1024)} %broadcast_multiply_fusion.6, ...), channel_id=2, replica_groups=mesh['replica'=2,'fsdp'=16] {'fsdp'}, use_global_device_ids=true, to_apply=%region_12.13.clone | all-reduce | flops 9216 | bytes 73728
  679.1 5.7 all-reduce.17
  686.1 2.3 multiply_add_fusion
  688.4 4.2 fusion.18
  692.6 1.9 copy.73
  694.5 1.6 copy.74
  696.1 1.9 copy.75
  (141 shorter events, 43.1 us)
Async XLA Ops:
  7.2 80.8 %copy-start = (f32[192,768]{1,0:T(8,128)S(1)}, f32[192,768]{1,0:T(8,128)}, u32[]{:S(2)}) copy-start(f32[192,768]{1,0:T(8,128)} %param.15) | copy-start | bytes 1769476
  7.2 80.7 %all-gather.5.cloned.1.call-start = ((), (), s32[]{:S(2)}) async-start(), calls=%async_computation.4 | async-start | bytes 3760128 | tf_op jit(solution)/shard_map/all_gather | solution.py:68
  7.9 91.9 %all-gather.7.cloned.1.call-start = ((), (), s32[]{:S(2)}) async-start(), calls=%async_computation.5 | async-start | bytes 1253376 | tf_op jit(solution)/shard_map/all_gather | solution.py:70
  8.7 145.4 %all-gather.9.cloned.1.call-start = ((), (), s32[]{:S(2)}) async-start(), calls=%async_computation.6 | async-start | bytes 5013504 | tf_op jit(solution)/shard_map/all_gather | solution.py:74
  9.4 198.5 %all-gather.11.cloned.1.call-start = ((), (), s32[]{:S(2)}) async-start(), calls=%async_computation.7 | async-start | bytes 5013504 | tf_op jit(solution)/shard_map/all_gather | solution.py:76
  10.0 270.8 %reduce-scatter.7.cloned.1.call-start = ((), (), s32[]{:S(2)}) async-start(), calls=%async_computation.9 | async-start | bytes 2506752 | tf_op jit(solution)/shard_map/reduce_scatter | solution.py:190
  85.7 5.2 copy-start.20
  87.0 3.9 copy-start.23
  87.9 4.9 copy-start.12
  91.2 1.6 copy-start.9
  92.2 1.4 copy-start.2
  92.8 1.6 copy-start.28
  94.4 8.0 %copy-start.6 = (bf16[12,64,192]{2,1,0:T(8,128)(2,1)}, bf16[12,64,192]{2,1,0:T(8,128)(2,1)S(1)}, u32[]{:S(2)}) copy-start(bf16[12,64,192]{2,1,0:T(8,128)(2,1)S(1)} %convolution_convert_fusion) | copy-start | bytes 884740
  208.0 5.0 copy-start.1
  208.0 5.0 copy-start.17
  208.0 5.0 copy-start.19
  212.9 2.4 copy-start.5
  212.9 2.4 copy-start.4
  215.3 1.7 copy-start.7
  218.9 154.8 %reduce-scatter.5.cloned.1.call-start = ((), (), s32[]{:S(2)}) async-start(), calls=%async_computation.8 | async-start | bytes 7520256 | tf_op jit(solution)/shard_map/reduce_scatter | solution.py:188
  240.4 4.1 copy-start.13
  240.4 4.1 copy-start.14
  240.4 4.1 copy-start.21
  240.4 4.1 copy-start.24
  248.7 240.0 %reduce-scatter.9.cloned.1.call-start = ((), (), s32[]{:S(2)}) async-start(), calls=%async_computation.10 | async-start | bytes 10027008 | tf_op jit(solution)/shard_map/reduce_scatter | solution.py:194
  255.8 347.8 %reduce-scatter.11.cloned.1.call-start = ((), (), s32[]{:S(2)}) async-start(), calls=%async_computation.11 | async-start | bytes 10027008 | tf_op jit(solution)/shard_map/reduce_scatter | solution.py:196
  262.0 5.4 copy-start.22
  262.0 5.4 copy-start.25
  262.1 430.5 %all-reduce.22.cloned.1.call-start = ((), (), s32[]{:S(2)}) async-start(), calls=%async_computation.12 | async-start | bytes 3538944 | tf_op jit(solution)/shard_map/psum | solution.py:199
  267.5 6.4 copy-start.27
  267.5 7.0 copy-start.26
  692.6 5.4 copy-start.11
  (6 other events, 5.6 us)
Sparse Core Ops, SparseCore 0:
  10.3 50.2 all-gather.4
  62.9 36.8 all-gather.6
  102.1 51.9 all-gather.8
  156.2 51.6 all-gather.10
  219.0 61.7 reduce-scatter.6
  284.7 88.9 reduce-scatter.4
  377.8 110.8 reduce-scatter.8
  492.8 110.8 reduce-scatter.10
  606.1 55.5 all-reduce.21
where the time goes:
time: 707 us; the launch traced here: 705 us
  waiting for transfers between devices  439 us (62%)
  blocking collectives  131 us (19%)
  matrix products  67.7 us (10%)
  local copies, waits for them, and re-layouts  32.6 us (5%)
  between operations  18.1 us (3%)
  other arithmetic  16.8 us (2%)
    unnamed x2, blocking collectives  125 us
    reduce_scatter x1, waiting for transfers between devices, on_device(): lax.psum_scatter(mats[3], 'fsdp', scatter_dimension=0, tiled=True)  115 us
    reduce_scatter x1, waiting for transfers between devices, on_device(): lax.psum_scatter(mats[2], 'fsdp', scatter_dimension=0, tiled=True)  115 us
    reduce_scatter x1, waiting for transfers between devices, on_device(): lax.psum_scatter(mats[0], 'fsdp', scatter_dimension=0, tiled=True)  92.9 us
    all_gather x1, waiting for transfers between devices, on_device(): lax.all_gather(fc1_weight, 'fsdp', axis=0, tiled=True)  51.7 us
    all_gather x1, waiting for transfers between devices, on_device(): lax.all_gather(fc2_weight, 'fsdp', axis=0, tiled=True)  50.3 us
    unnamed x87, local copies, waits for them, and re-layouts  27.5 us
    dot_general x4, matrix products, on_device(): jnp.dot(left.T, right, preferred_element_type=f32) * factor  18.7 us
  transfers between devices with their start and end apart: 9, of which 7 were waited for; matrix products, arithmetic and copies ran while one was open for 14% of the time, Pallas kernels for 0%

commit v1 on v0

--- a/solution.py
+++ b/solution.py
@@ -8,6 +8,18 @@
 HEAD_DIM = 64
 L = 192
 EPSILON = 1e-05
+
+
+def gather_around(shard, axis, dim):
+    ways, here, turn = (lax.axis_size(axis), lax.axis_index(axis), shard.shape[dim])
+    dims = [n * ways if d == dim else n for d, n in enumerate(shard.shape)]
+    full = lax.dynamic_update_slice_in_dim(
+        jnp.zeros(dims, shard.dtype), shard, here * turn, axis=dim
+    )
+    for far in range(1, ways):
+        shard = lax.ppermute(shard, axis, [(d, (d + 1) % ways) for d in range(ways)])
+        full = lax.dynamic_update_slice_in_dim(full, shard, (here - far) % ways * turn, axis=dim)
+    return full
 
 
 def layer_norm(inputs, gain_vec, shift_vec):
@@ -73,7 +85,7 @@
         lax.all_gather(norm2_shift, "fsdp", axis=0, tiled=True),
         lax.all_gather(fc1_weight, "fsdp", axis=0, tiled=True),
         lax.all_gather(fc1_bias, "fsdp", axis=0, tiled=True),
-        lax.all_gather(fc2_weight, "fsdp", axis=0, tiled=True),
+        gather_around(fc2_weight, "fsdp", 0),
         lax.all_gather(fc2_bias, "fsdp", axis=0, tiled=True),
     )
     (

time: 707 us -> 719 us (1.017)
  local copies, waits for them, and re-layouts: 32.6 us -> 61.4 us
  waiting for transfers between devices: 439 us -> 421 us
    ppermute x0 -> x15, waiting for transfers between devices: none -> 130 us  [gather_around(): lax.ppermute(shard, axis, [(d, (d + 1) % ways) for d in range(ways)])]
    reduce_scatter x1, waiting for transfers between devices: 92.9 us -> 0.01 us  [on_device(): lax.psum_scatter(mats[0], 'fsdp', scatter_dimension=0, tiled=True)]
    reduce_scatter x1, waiting for transfers between devices: 115 us -> 68.9 us  [on_device(): lax.psum_scatter(mats[2], 'fsdp', scatter_dimension=0, tiled=True)]
    dynamic_update_slice x0 -> x16, local copies, waits for them, and re-layouts: none -> 18.6 us  [the longest x15 17.9 us: gather_around(): lax.dynamic_update_slice_in_dim(full, shard, (here - far) % ways * turn,...]
    unnamed x87 -> x113, local copies, waits for them, and re-layouts: 27.5 us -> 31.8 us
  transfers between devices with their start and end apart: 9 -> 24, of which waited for: 7 -> 20; matrix products, arithmetic and copies ran while one was open for 14% -> 17% of each run, Pallas kernels for 0% -> 0%
where the time goes in v1:
time: 719 us; the launch traced here: 717 us
  waiting for transfers between devices  421 us (59%)
  blocking collectives  131 us (18%)
  matrix products  68.6 us (10%)
  local copies, waits for them, and re-layouts  61.4 us (9%)
  between operations  18.2 us (3%)
  other arithmetic  16 us (2%)
    ppermute x15, waiting for transfers between devices, gather_around(): lax.ppermute(shard, axis, [(d, (d + 1) % ways) for d in range(ways)])  130 us
    unnamed x2, blocking collectives  125 us
    reduce_scatter x1, waiting for transfers between devices, on_device(): lax.psum_scatter(mats[3], 'fsdp', scatter_dimension=0, tiled=True)  115 us
    reduce_scatter x1, waiting for transfers between devices, on_device(): lax.psum_scatter(mats[2], 'fsdp', scatter_dimension=0, tiled=True)  68.9 us
    all_gather x1, waiting for transfers between devices, on_device(): lax.all_gather(fc1_weight, 'fsdp', axis=0, tiled=True)  51.7 us
    all_gather x1, waiting for transfers between devices, on_device(): lax.all_gather(fc2_weight, 'fsdp', axis=0, tiled=True)  50.3 us
    unnamed x113, local copies, waits for them, and re-layouts  31.8 us
    dot_general x4, matrix products, on_device(): jnp.dot(left.T, right, preferred_element_type=f32) * factor  18.7 us
  transfers between devices with their start and end apart: 24, of which 20 were waited for; matrix products, arithmetic and copies ran while one was open for 17% of the time, Pallas kernels for 0%

profile of v1, /device:TPU:0, one launch (start us, length us, event | category | flops | bytes accessed | tf_op | source)
XLA Modules:
  0.0 716.9 jit_solution(11355789152999619735)
XLA Ops:
  20.0 63.8 %all-reduce.19 = (bf16[768]{0:T(1024)(128)(2,1)S(1)}, bf16[768]{0:T(1024)(128)(2,1)S(1)}, bf16[1536]{0:T(1024)(128)(2,1)S(1)}, bf16[768]{0:T(1024)(128)(2,1)S(1)...) all-reduce(bf16[768]{0:T(1024)(128)(2,1)S(1)} %dynamic-update-slice, ...), channel_id=1, replica_groups=mesh['replica'=2,'fsdp'=16] {'fsdp'}, use_global_device_ids=true, to_apply=%add.1 | all-reduce | flops 9216 | bytes 36864
  102.7 51.7 %all-gather.9.cloned.1.call-done = bf16[768,3072]{1,0:T(8,128)(2,1)} async-done(((bf16[48,3072]{1,0:T(8,128)(2,1)}), bf16[768,3072]{1,0:T(8,128)(2,1)}) %all-gather.9.cloned.1.call-update) | async-done | bytes 4718608 | tf_op jit(solution)/shard_map/all_gather | solution.py:86
  154.4 3.5 convolution_add_fusion
  157.9 50.3 %all-gather.11.cloned.1.call-done = bf16[3072,768]{1,0:T(8,128)(2,1)} async-done(((bf16[192,768]{1,0:T(8,128)(2,1)}), bf16[3072,768]{1,0:T(8,128)(2,1)}) %all-gather.11.cloned.1.call-update) | async-done | bytes 4718608 | tf_op jit(solution)/shard_map/all_gather | solution.py:138
  208.2 4.9 fusion.51
  227.0 7.1 fusion.44
  234.1 6.4 fusion.15
  240.6 3.3 fusion.45
  244.6 4.2 convolution_multiply_fusion
  249.5 6.5 convolution_multiply_fusion.2
  256.0 6.2 convolution_multiply_fusion.1
  262.6 8.9 %collective-permute-done = bf16[192,768]{1,0:T(8,128)(2,1)S(1)} collective-permute-done((bf16[192,768]{1,0:T(8,128)(2,1)}, bf16[192,768]{1,0:T(8,128)(2,1)S(1)}, u32[]{:S(2)}, u32[]{:S(2)}) %collective-permute-start) | collective-permute-done | bytes 294944 | tf_op jit(solution)/shard_map/ppermute | solution.py:20
  272.2 10.0 %collective-permute-done.1 = bf16[192,768]{1,0:T(8,128)(2,1)S(1)} collective-permute-done((bf16[192,768]{1,0:T(8,128)(2,1)S(1)}, bf16[192,768]{1,0:T(8,128)(2,1)S(1)}, u32[]{:S(2)}, u32[]{:S(2)}) %collective-permute-start.1) | collective-permute-done | bytes 294944 | tf_op jit(solution)/shard_map/ppermute | solution.py:20
  282.9 8.1 %collective-permute-done.2 = bf16[192,768]{1,0:T(8,128)(2,1)S(1)} collective-permute-done((bf16[192,768]{1,0:T(8,128)(2,1)S(1)}, bf16[192,768]{1,0:T(8,128)(2,1)S(1)}, u32[]{:S(2)}, u32[]{:S(2)}) %collective-permute-start.2) | collective-permute-done | bytes 294944 | tf_op jit(solution)/shard_map/ppermute | solution.py:20
  291.8 8.8 %collective-permute-done.3 = bf16[192,768]{1,0:T(8,128)(2,1)S(1)} collective-permute-done((bf16[192,768]{1,0:T(8,128)(2,1)S(1)}, bf16[192,768]{1,0:T(8,128)(2,1)S(1)}, u32[]{:S(2)}, u32[]{:S(2)}) %collective-permute-start.3) | collective-permute-done | bytes 294944 | tf_op jit(solution)/shard_map/ppermute | solution.py:20
  300.6 8.8 %collective-permute-done.4 = bf16[192,768]{1,0:T(8,128)(2,1)S(1)} collective-permute-done((bf16[192,768]{1,0:T(8,128)(2,1)S(1)}, bf16[192,768]{1,0:T(8,128)(2,1)S(1)}, u32[]{:S(2)}, u32[]{:S(2)}) %collective-permute-start.4) | collective-permute-done | bytes 294944 | tf_op jit(solution)/shard_map/ppermute | solution.py:20
  310.2 8.2 %collective-permute-done.5 = bf16[192,768]{1,0:T(8,128)(2,1)S(1)} collective-permute-done((bf16[192,768]{1,0:T(8,128)(2,1)S(1)}, bf16[192,768]{1,0:T(8,128)(2,1)S(1)}, u32[]{:S(2)}, u32[]{:S(2)}) %collective-permute-start.5) | collective-permute-done | bytes 294944 | tf_op jit(solution)/shard_map/ppermute | solution.py:20
  319.1 15.3 %collective-permute-done.6 = bf16[192,768]{1,0:T(8,128)(2,1)S(1)} collective-permute-done((bf16[192,768]{1,0:T(8,128)(2,1)S(1)}, bf16[192,768]{1,0:T(8,128)(2,1)S(1)}, u32[]{:S(2)}, u32[]{:S(2)}) %collective-permute-start.6) | collective-permute-done | bytes 294944 | tf_op jit(solution)/shard_map/ppermute | solution.py:20
  335.2 9.5 %collective-permute-done.7 = bf16[192,768]{1,0:T(8,128)(2,1)S(1)} collective-permute-done((bf16[192,768]{1,0:T(8,128)(2,1)S(1)}, bf16[192,768]{1,0:T(8,128)(2,1)S(1)}, u32[]{:S(2)}, u32[]{:S(2)}) %collective-permute-start.7) | collective-permute-done | bytes 294944 | tf_op jit(solution)/shard_map/ppermute | solution.py:20
  345.4 14.4 %collective-permute-done.8 = bf16[192,768]{1,0:T(8,128)(2,1)} collective-permute-done((bf16[192,768]{1,0:T(8,128)(2,1)S(1)}, bf16[192,768]{1,0:T(8,128)(2,1)}, u32[]{:S(2)}, u32[]{:S(2)}) %collective-permute-start.8) | collective-permute-done | bytes 294944 | tf_op jit(solution)/shard_map/ppermute | solution.py:20
  359.9 9.4 %collective-permute-done.9 = bf16[192,768]{1,0:T(8,128)(2,1)} collective-permute-done((bf16[192,768]{1,0:T(8,128)(2,1)}, bf16[192,768]{1,0:T(8,128)(2,1)}, u32[]{:S(2)}, u32[]{:S(2)}) %collective-permute-start.9) | collective-permute-done | bytes 294944 | tf_op jit(solution)/shard_map/ppermute | solution.py:20
  378.1 6.8 collective-permute-done.10
  389.0 4.9 collective-permute-done.11
  396.1 6.6 collective-permute-done.12
  407.9 3.7 collective-permute-done.13
  413.8 6.7 collective-permute-done.14
  423.9 5.1 multiply_reduce_fusion.2
  431.4 68.9 %reduce-scatter.9.cloned.1.call-done = f32[48,3072]{1,0:T(8,128)} async-done(((f32[768,3072]{1,0:T(8,128)}), f32[48,3072]{1,0:T(8,128)}) %reduce-scatter.9.cloned.1.call-update) | async-done | bytes 589840 | tf_op jit(solution)/shard_map/reduce_scatter | solution.py:206
  500.3 115.0 %reduce-scatter.11.cloned.1.call-done = f32[192,768]{1,0:T(8,128)} async-done(((f32[3072,768]{1,0:T(8,128)}), f32[192,768]{1,0:T(8,128)}) %reduce-scatter.11.cloned.1.call-update) | async-done | bytes 589840 | tf_op jit(solution)/shard_map/reduce_scatter | solution.py:208
  619.2 61.4 %all-reduce.16 = (f32[768]{0:T(1024)}, f32[768]{0:T(1024)}, f32[1536]{0:T(1024)}, f32[768]{0:T(1024)}, f32[768]{0:T(1024)}, /*index=5*/f32[768]{0:T(1024)}, f32[3072]{0:T(1024)}, f32[768]{0:T(1024)}) all-reduce(f32[768]{0:T(1024)} %broadcast_multiply_fusion.6, ...), channel_id=2, replica_groups=mesh['replica'=2,'fsdp'=16] {'fsdp'}, use_global_device_ids=true, to_apply=%region_12.13.clone | all-reduce | flops 9216 | bytes 73728
  690.8 5.7 all-reduce.17
  700.0 4.2 fusion.18
  (214 shorter events, 100.3 us)
Async XLA Ops:
  7.2 80.8 %copy-start = (f32[192,768]{1,0:T(8,128)S(1)}, f32[192,768]{1,0:T(8,128)}, u32[]{:S(2)}) copy-start(f32[192,768]{1,0:T(8,128)} %param.15) | copy-start | bytes 1769476
  7.2 80.7 %all-gather.5.cloned.1.call-start = ((), (), s32[]{:S(2)}) async-start(), calls=%async_computation.4 | async-start | bytes 3760128 | tf_op jit(solution)/shard_map/all_gather | solution.py:80
  7.9 92.1 %all-gather.7.cloned.1.call-start = ((), (), s32[]{:S(2)}) async-start(), calls=%async_computation.5 | async-start | bytes 1253376 | tf_op jit(solution)/shard_map/all_gather | solution.py:82
  8.7 145.7 %all-gather.9.cloned.1.call-start = ((), (), s32[]{:S(2)}) async-start(), calls=%async_computation.6 | async-start | bytes 5013504 | tf_op jit(solution)/shard_map/all_gather | solution.py:86
  9.4 198.8 %all-gather.11.cloned.1.call-start = ((), (), s32[]{:S(2)}) async-start(), calls=%async_computation.7 | async-start | bytes 5013504 | tf_op jit(solution)/shard_map/all_gather | solution.py:138
  10.0 421.4 %reduce-scatter.7.cloned.1.call-start = ((), (), s32[]{:S(2)}) async-start(), calls=%async_computation.9 | async-start | bytes 2506752 | tf_op jit(solution)/shard_map/reduce_scatter | solution.py:202
  219.1 212.3 %reduce-scatter.5.cloned.1.call-start = ((), (), s32[]{:S(2)}) async-start(), calls=%async_computation.8 | async-start | bytes 7520256 | tf_op jit(solution)/shard_map/reduce_scatter | solution.py:200
  248.9 251.4 %reduce-scatter.9.cloned.1.call-start = ((), (), s32[]{:S(2)}) async-start(), calls=%async_computation.10 | async-start | bytes 10027008 | tf_op jit(solution)/shard_map/reduce_scatter | solution.py:206
  256.0 359.3 %reduce-scatter.11.cloned.1.call-start = ((), (), s32[]{:S(2)}) async-start(), calls=%async_computation.11 | async-start | bytes 10027008 | tf_op jit(solution)/shard_map/reduce_scatter | solution.py:208
  262.2 442.0 %all-reduce.22.cloned.1.call-start = ((), (), s32[]{:S(2)}) async-start(), calls=%async_computation.12 | async-start | bytes 3538944 | tf_op jit(solution)/shard_map/psum | solution.py:211
  262.3 9.2 %collective-permute-start = (bf16[192,768]{1,0:T(8,128)(2,1)}, bf16[192,768]{1,0:T(8,128)(2,1)S(1)}, u32[]{:S(2)}, u32[]{:S(2)}) collective-permute-start(bf16[192,768]{1,0:T(8,128)(2,1)} %param.28), channel_id=1, source_target_pairs={{0,1},{1,2},{2,3},{3,4},{4,5},{5,6},{6,7},{7,8},{8,9},{9,10},{10,1... | collective-permute-start | bytes 884744 | tf_op jit(solution)/shard_map/ppermute | solution.py:20
  271.5 10.7 %collective-permute-start.1 = (bf16[192,768]{1,0:T(8,128)(2,1)S(1)}, bf16[192,768]{1,0:T(8,128)(2,1)S(1)}, u32[]{:S(2)}, u32[]{:S(2)}) collective-permute-start(bf16[192,768]{1,0:T(8,128)(2,1)S(1)} %collective-permute-done), channel_id=1, source_target_pairs={{0,1},{1,2},{2,3},{3,4},{4,5},{5,6},{6,7},{7,8},{8,9},{9,10},{10,1... | collective-permute-start | bytes 884744 | tf_op jit(solution)/shard_map/ppermute | solution.py:20
  282.2 8.8 %collective-permute-start.2 = (bf16[192,768]{1,0:T(8,128)(2,1)S(1)}, bf16[192,768]{1,0:T(8,128)(2,1)S(1)}, u32[]{:S(2)}, u32[]{:S(2)}) collective-permute-start(bf16[192,768]{1,0:T(8,128)(2,1)S(1)} %collective-permute-done.1), channel_id=1, source_target_pairs={{0,1},{1,2},{2,3},{3,4},{4,5},{5,6},{6,7},{7,8},{8,9},{9,10},{10,1... | collective-permute-start | bytes 884744 | tf_op jit(solution)/shard_map/ppermute | solution.py:20
  291.8 8.8 %collective-permute-start.3 = (bf16[192,768]{1,0:T(8,128)(2,1)S(1)}, bf16[192,768]{1,0:T(8,128)(2,1)S(1)}, u32[]{:S(2)}, u32[]{:S(2)}) collective-permute-start(bf16[192,768]{1,0:T(8,128)(2,1)S(1)} %collective-permute-done.2), channel_id=1, source_target_pairs={{0,1},{1,2},{2,3},{3,4},{4,5},{5,6},{6,7},{7,8},{8,9},{9,10},{10,1... | collective-permute-start | bytes 884744 | tf_op jit(solution)/shard_map/ppermute | solution.py:20
  300.6 33.8 %copy-start.20 = (bf16[192,768]{1,0:T(8,128)(2,1)}, bf16[192,768]{1,0:T(8,128)(2,1)S(1)}, u32[]{:S(2)}) copy-start(bf16[192,768]{1,0:T(8,128)(2,1)S(1)} %collective-permute-done.3) | copy-start | bytes 884740
  300.6 8.8 %collective-permute-start.4 = (bf16[192,768]{1,0:T(8,128)(2,1)S(1)}, bf16[192,768]{1,0:T(8,128)(2,1)S(1)}, u32[]{:S(2)}, u32[]{:S(2)}) collective-permute-start(bf16[192,768]{1,0:T(8,128)(2,1)S(1)} %collective-permute-done.3), channel_id=1, source_target_pairs={{0,1},{1,2},{2,3},{3,4},{4,5},{5,6},{6,7},{7,8},{8,9},{9,10},{10,1... | collective-permute-start | bytes 884744 | tf_op jit(solution)/shard_map/ppermute | solution.py:20
  309.5 8.9 %collective-permute-start.5 = (bf16[192,768]{1,0:T(8,128)(2,1)S(1)}, bf16[192,768]{1,0:T(8,128)(2,1)S(1)}, u32[]{:S(2)}, u32[]{:S(2)}) collective-permute-start(bf16[192,768]{1,0:T(8,128)(2,1)S(1)} %collective-permute-done.4), channel_id=1, source_target_pairs={{0,1},{1,2},{2,3},{3,4},{4,5},{5,6},{6,7},{7,8},{8,9},{9,10},{10,1... | collective-permute-start | bytes 884744 | tf_op jit(solution)/shard_map/ppermute | solution.py:20
  319.1 15.3 %collective-permute-start.6 = (bf16[192,768]{1,0:T(8,128)(2,1)S(1)}, bf16[192,768]{1,0:T(8,128)(2,1)S(1)}, u32[]{:S(2)}, u32[]{:S(2)}) collective-permute-start(bf16[192,768]{1,0:T(8,128)(2,1)S(1)} %collective-permute-done.5), channel_id=1, source_target_pairs={{0,1},{1,2},{2,3},{3,4},{4,5},{5,6},{6,7},{7,8},{8,9},{9,10},{10,1... | collective-permute-start | bytes 884744 | tf_op jit(solution)/shard_map/ppermute | solution.py:20
  334.4 10.2 %collective-permute-start.7 = (bf16[192,768]{1,0:T(8,128)(2,1)S(1)}, bf16[192,768]{1,0:T(8,128)(2,1)S(1)}, u32[]{:S(2)}, u32[]{:S(2)}) collective-permute-start(bf16[192,768]{1,0:T(8,128)(2,1)S(1)} %collective-permute-done.6), channel_id=1, source_target_pairs={{0,1},{1,2},{2,3},{3,4},{4,5},{5,6},{6,7},{7,8},{8,9},{9,10},{10,1... | collective-permute-start | bytes 884744 | tf_op jit(solution)/shard_map/ppermute | solution.py:20
  345.4 14.4 %collective-permute-start.8 = (bf16[192,768]{1,0:T(8,128)(2,1)S(1)}, bf16[192,768]{1,0:T(8,128)(2,1)}, u32[]{:S(2)}, u32[]{:S(2)}) collective-permute-start(bf16[192,768]{1,0:T(8,128)(2,1)S(1)} %collective-permute-done.7), channel_id=1, source_target_pairs={{0,1},{1,2},{2,3},{3,4},{4,5},{5,6},{6,7},{7,8},{8,9},{9,10},{10,1... | collective-permute-start | bytes 884744 | tf_op jit(solution)/shard_map/ppermute | solution.py:20
  359.8 9.4 %collective-permute-start.9 = (bf16[192,768]{1,0:T(8,128)(2,1)}, bf16[192,768]{1,0:T(8,128)(2,1)}, u32[]{:S(2)}, u32[]{:S(2)}) collective-permute-start(bf16[192,768]{1,0:T(8,128)(2,1)} %collective-permute-done.8), channel_id=1, source_target_pairs={{0,1},{1,2},{2,3},{3,4},{4,5},{5,6},{6,7},{7,8},{8,9},{9,10},{10,1... | collective-permute-start | bytes 884744 | tf_op jit(solution)/shard_map/ppermute | solution.py:20
  359.9 14.6 %copy-start.41 = (bf16[768]{0:T(1024)(128)(2,1)S(1)}, bf16[768]{0:T(1024)(128)(2,1)}, u32[]{:S(2)}) copy-start(bf16[768]{0:T(1024)(128)(2,1)} %get-tuple-element.49) | copy-start | bytes 4612
  369.2 15.6 %collective-permute-start.10 = (bf16[192,768]{1,0:T(8,128)(2,1)}, bf16[192,768]{1,0:T(8,128)(2,1)}, u32[]{:S(2)}, u32[]{:S(2)}) collective-permute-start(bf16[192,768]{1,0:T(8,128)(2,1)} %collective-permute-done.9), channel_id=1, source_target_pairs={{0,1},{1,2},{2,3},{3,4},{4,5},{5,6},{6,7},{7,8},{8,9},{9,10},{10,1... | collective-permute-start | bytes 884744 | tf_op jit(solution)/shard_map/ppermute | solution.py:20
  374.6 19.3 %copy-start.19 = (bf16[192,768]{1,0:T(8,128)(2,1)S(1)}, bf16[192,768]{1,0:T(8,128)(2,1)}, u32[]{:S(2)}) copy-start(bf16[192,768]{1,0:T(8,128)(2,1)} %copy-done.18) | copy-start | bytes 884740
  374.6 20.0 %copy-start.23 = (bf16[192,768]{1,0:T(8,128)(2,1)S(1)}, bf16[192,768]{1,0:T(8,128)(2,1)}, u32[]{:S(2)}) copy-start(bf16[192,768]{1,0:T(8,128)(2,1)} %copy-done.22) | copy-start | bytes 884740
  374.6 20.8 %copy-start.27 = (bf16[192,768]{1,0:T(8,128)(2,1)S(1)}, bf16[192,768]{1,0:T(8,128)(2,1)}, u32[]{:S(2)}) copy-start(bf16[192,768]{1,0:T(8,128)(2,1)} %copy-done.26) | copy-start | bytes 884740
  384.8 9.1 %collective-permute-start.11 = (bf16[192,768]{1,0:T(8,128)(2,1)}, bf16[192,768]{1,0:T(8,128)(2,1)S(1)}, u32[]{:S(2)}, u32[]{:S(2)}) collective-permute-start(bf16[192,768]{1,0:T(8,128)(2,1)} %collective-permute-done.10), channel_id=1, source_target_pairs={{0,1},{1,2},{2,3},{3,4},{4,5},{5,6},{6,7},{7,8},{8,9},{9,10},{10,1... | collective-permute-start | bytes 884744 | tf_op jit(solution)/shard_map/ppermute | solution.py:20
  393.9 8.8 %collective-permute-start.12 = (bf16[192,768]{1,0:T(8,128)(2,1)S(1)}, bf16[192,768]{1,0:T(8,128)(2,1)S(1)}, u32[]{:S(2)}, u32[]{:S(2)}) collective-permute-start(bf16[192,768]{1,0:T(8,128)(2,1)S(1)} %collective-permute-done.11), channel_id=1, source_target_pairs={{0,1},{1,2},{2,3},{3,4},{4,5},{5,6},{6,7},{7,8},{8,9},{9,10},{10,1... | collective-permute-start | bytes 884744 | tf_op jit(solution)/shard_map/ppermute | solution.py:20
  395.3 28.5 %copy-start.34 = (f32[192]{0:T(256)S(1)}, f32[192]{0:T(256)}, u32[]{:S(2)}) copy-start(f32[192]{0:T(256)} %copy-done.32) | copy-start | bytes 2308
  395.4 28.5 %copy-start.37 = (f32[192]{0:T(256)S(1)}, f32[192]{0:T(256)}, u32[]{:S(2)}) copy-start(f32[192]{0:T(256)} %copy-done.35) | copy-start | bytes 2308
  402.7 8.8 %collective-permute-start.13 = (bf16[192,768]{1,0:T(8,128)(2,1)S(1)}, bf16[192,768]{1,0:T(8,128)(2,1)S(1)}, u32[]{:S(2)}, u32[]{:S(2)}) collective-permute-start(bf16[192,768]{1,0:T(8,128)(2,1)S(1)} %collective-permute-done.12), channel_id=1, source_target_pairs={{0,1},{1,2},{2,3},{3,4},{4,5},{5,6},{6,7},{7,8},{8,9},{9,10},{10,1... | collective-permute-start | bytes 884744 | tf_op jit(solution)/shard_map/ppermute | solution.py:20
  411.6 8.8 %collective-permute-start.14 = (bf16[192,768]{1,0:T(8,128)(2,1)S(1)}, bf16[192,768]{1,0:T(8,128)(2,1)S(1)}, u32[]{:S(2)}, u32[]{:S(2)}) collective-permute-start(bf16[192,768]{1,0:T(8,128)(2,1)S(1)} %collective-permute-done.13), channel_id=1, source_target_pairs={{0,1},{1,2},{2,3},{3,4},{4,5},{5,6},{6,7},{7,8},{8,9},{9,10},{10,1... | collective-permute-start | bytes 884744 | tf_op jit(solution)/shard_map/ppermute | solution.py:20
  (34 other events, 122.6 us)
Sparse Core Ops, SparseCore 0:
  10.3 50.5 all-gather.4
  63.1 36.8 all-gather.6
  102.3 51.9 all-gather.8
  156.5 51.6 all-gather.10
  219.3 61.8 reduce-scatter.6
  285.0 97.4 reduce-scatter.4
  386.6 113.5 reduce-scatter.8
  504.4 110.8 reduce-scatter.10
  617.8 55.5 all-reduce.21
